TPU v7x, 32 devices: a whole 2x2x4 slice. The times are simulated.
32 devices in a mesh: row: 4 (over x, core), col: 8 (over z, y).
Axes of the slice: x: 2, y: 2, z: 4, core: 2. Of those that a mesh axis runs over, the one named last changes fastest.
Arguments:
- panel: bfloat16 [3072, 98304], P('row', 'col'), may hold values from -0.01953125 to 0.01953125
- surface: bfloat16 [98304, 1024], P('col'), may hold values from -6 to 6
- flexibility: float32 [4, 768, 768], P('row'), may hold values from -0.21875 to 0.21875
- owner_map: int32 [24], replicated, may hold values from 0 to 23, each once
- adjacency: int32 [4, 2], P('row'), may hold values from 0 to 3, as said below
- live_rows: int32 [24], replicated, may hold values from 1 to 128, 2304 in all
Outputs:
- response: float32 [1024, 98304], P('row', 'col')
Inputs may be any that keep to these rules, and one draw needn't show every extreme that they name: `adjacency`: each substructure lists 2 different neighbours, never itself. `owner_map`: every slot receives exactly one mortar block. `live_rows`: the live rows add up to 2304 and some block is full.
All inputs are finite; a program needn't handle non-finite values.
Results may differ from a plain program's by a relative error of at most 0.0029.
Values may be sent and summed in bfloat16 or wider, within the bound.
A program may use at most 192 MiB of HBM per device.

v0:
```python
import math
import jax
import jax.numpy as jnp
from jax import lax
from jax.sharding import PartitionSpec as P

MBLK = 128
ITERS = 2
DAMPING = 0.6
COUPLING = 0.5


def live_pattern(live_rows):
    offsets = jnp.arange(MBLK, dtype=jnp.int32)
    return (offsets[None, :] < live_rows[:, None]).astype(jnp.float32)


def body(panel, surface, flexibility, owner_map, adjacency, live_rows):
    order_rows, column_count = panel.shape
    row_total = lax.axis_size("row")
    col_total = lax.axis_size("col")
    own_row = lax.axis_index("row")
    load_total = surface.shape[1]
    load_share = load_total // col_total
    block_count = order_rows // MBLK
    traction = lax.psum_scatter(
        lax.dot_general(
            surface, panel, (((0,), (1,)), ((), ())), preferred_element_type=jnp.float32
        ),
        "col",
        scatter_dimension=0,
        tiled=True,
    )
    pattern = live_pattern(live_rows)
    own_pattern = lax.dynamic_slice_in_dim(pattern, own_row * block_count, block_count, 0)
    blocks = traction.reshape(load_share, block_count, MBLK) * own_pattern[None]
    every_block = lax.all_gather(blocks, "row", axis=1, tiled=True)
    block_total = owner_map.shape[0]
    inverse = (
        jnp.zeros((block_total,), jnp.int32)
        .at[owner_map]
        .set(jnp.arange(block_total, dtype=jnp.int32))
    )
    own_sources = lax.dynamic_slice_in_dim(inverse, own_row * block_count, block_count, 0)
    load_blocks = jnp.take(every_block, own_sources, axis=1).reshape(load_share, order_rows)
    hits = adjacency[0][:, None] == jnp.arange(row_total, dtype=jnp.int32)[None, :]
    neighbour_weights = jnp.sum(hits.astype(jnp.float32), axis=0)
    flex_local = flexibility[0]
    traces = jnp.zeros_like(load_blocks)
    for sweep_index in range(ITERS):
        coupled = load_blocks
        if sweep_index > 0:
            neighbours = lax.all_gather(traces[None], "row", axis=0, tiled=True)
            coupled = load_blocks + COUPLING * jnp.einsum(
                "n,nlo->lo", neighbour_weights, neighbours, precision=lax.Precision.HIGHEST
            )
        applied = lax.dot_general(
            coupled,
            flex_local,
            (((1,), (1,)), ((), ())),
            precision=lax.Precision.HIGHEST,
            preferred_element_type=jnp.float32,
        )
        traces = (1.0 - DAMPING) * traces + DAMPING * applied
    rounded = traces.astype(jnp.bfloat16).reshape(load_share, block_count, MBLK)
    every_trace = lax.all_gather(rounded, "row", axis=1, tiled=True)
    own_slots = lax.dynamic_slice_in_dim(owner_map, own_row * block_count, block_count, 0)
    updated = (
        jnp.take(every_trace, own_slots, axis=1) * own_pattern[None].astype(jnp.bfloat16)
    ).reshape(load_share, order_rows)
    all_loads = lax.all_gather(updated, "col", axis=0, tiled=True)
    gain_factor = math.sqrt(column_count * col_total / (order_rows * row_total))
    return lax.psum_scatter(
        gain_factor * jnp.dot(all_loads, panel, preferred_element_type=jnp.float32),
        "row",
        scatter_dimension=0,
        tiled=True,
    )


def solution(mesh):
    in_specs = (P("row", "col"), P("col", None), P("row", None, None), P(), P("row", None), P())
    out_specs = P("row", "col")
    return jax.shard_map(body, mesh=mesh, in_specs=in_specs, out_specs=out_specs, check_vma=False)
```

profile of v0, /device:TPU:0, one launch (start us, length us, event | category | flops | bytes accessed | tf_op | source)
XLA Modules:
  0.0 604.5 jit_solution(13668140794669306131)
XLA Ops:
  6.5 0.0 copy-start
  6.5 0.0 reduce-scatter.3.cloned.1.call-start
  6.5 26.5 %fusion.25 = f32[1024,768]{1,0:T(8,128)} fusion(bf16[12288,1024]{1,0:T(8,128)(2,1)} %param.7, bf16[768,12288]{1,0:T(8,128)(2,1)} %param.6), kind=kOutput, calls=%fused_computation.40 | convolution fusion | flops 19327352832 | bytes 47185920 | tf_op jit(solution)/shard_map/dot_general | solution.py:27
  33.0 0.0 copy-start.3
  33.0 0.0 copy-start.2
  33.0 0.0 reduce-scatter.3.cloned.1.call-update
  33.1 0.0 all-gather.5.cloned.1.call-start
  33.1 0.6 copy-done.3
  33.7 0.1 dynamic-slice
  33.8 0.1 convert_bitcast_fusion
  33.8 76.6 %reduce-scatter.3.cloned.1.call-done = f32[128,768]{1,0:T(8,128)} async-done(((f32[1024,768]{1,0:T(8,128)}), f32[128,768]{1,0:T(8,128)}) %reduce-scatter.3.cloned.1.call-update) | async-done | bytes 393232 | tf_op jit(solution)/shard_map/reduce_scatter | solution.py:26
  110.4 1.1 copy.21
  111.6 0.2 broadcast_multiply_fusion.1
  111.7 0.9 copy.22
  112.7 0.0 all-gather.5.cloned.1.call-update
  112.7 0.0 all-gather.9.cloned.1.call-start
  112.7 0.0 copy-done.2
  112.8 0.6 scatter_custom_fusion
  113.4 0.1 compare_and_fusion
  113.5 0.0 copy-start.4
  113.5 18.0 %all-gather.5.cloned.1.call-done = f32[128,24,128]{2,0,1:T(8,128)} async-done(((f32[128,6,128]{2,0,1:T(8,128)}), f32[128,24,128]{2,0,1:T(8,128)}) %all-gather.5.cloned.1.call-update) | async-done | bytes 1572880 | tf_op jit(solution)/shard_map/all_gather | solution.py:37
  131.6 2.0 gather_fusion
  133.6 0.1 broadcast_select_fusion
  133.7 0.2 copy.23
  133.8 0.0 copy-done
  133.8 2.8 broadcast_multiply_fusion
  136.7 0.0 all-gather.9.cloned.1.call-update
  136.7 0.2 all-gather.7.cloned.1.call-start
  136.9 0.1 compare_and_fusion.1
  137.0 0.0 copy-done.4
  137.0 0.7 fusion.20
  137.7 0.1 broadcast_bitcast_fusion
  137.8 0.1 broadcast_bitcast_fusion.1
  137.9 0.2 copy.24
  138.0 0.2 bitcast_select_fusion
  138.2 18.3 %all-gather.9.cloned.1.call-done = f32[512,768]{1,0:T(8,128)} async-done(((f32[128,768]{1,0:T(8,128)}), f32[512,768]{1,0:T(8,128)}) %all-gather.9.cloned.1.call-update) | async-done | bytes 1572880 | tf_op jit(solution)/shard_map/all_gather | solution.py:53
  156.5 5.7 fusion.4
  162.2 1.2 copy.29
  163.4 3.2 fusion.12
  166.6 1.1 copy.25
  167.7 0.2 copy.26
  167.9 8.6 %all_gather.14 = bf16[128,24,128]{2,0,1:T(8,128)(2,1)S(1)} all-gather(bf16[128,6,128]{2,0,1:T(8,128)(2,1)S(1)} %copy.26), channel_id=1, replica_groups=mesh['row'=4,'col'=8] {'row'}, dimensions={1}, use_global_device_ids=true | all-gather | bytes 983040 | tf_op jit(solution)/shard_map/all_gather | solution.py:66
  176.5 0.6 gather_fusion.1
  177.1 0.2 copy.27
  177.3 1.0 fusion.17
  178.2 0.0 all-gather.7.cloned.1.call-update
  178.2 0.3 reduce-scatter.5.cloned.1.call-start
  178.5 44.3 %all-gather.7.cloned.1.call-done = bf16[1024,768]{0,1:T(8,128)(2,1)} async-done(((bf16[128,768]{0,1:T(8,128)(2,1)}), bf16[1024,768]{0,1:T(8,128)(2,1)}) %all-gather.7.cloned.1.call-update) | async-done | bytes 1572880 | tf_op jit(solution)/shard_map/all_gather | solution.py:71
  222.8 30.3 %convolution_multiply_fusion = f32[1024,12288]{1,0:T(8,128)} fusion(bf16[1024,768]{0,1:T(8,128)(2,1)} %all-gather.7.cloned.1.call-done, bf16[768,12288]{1,0:T(8,128)(2,1)} %param.6), kind=kOutput, calls=%fused_computation.3 | convolution fusion | flops 19339935744 | bytes 70778880 | tf_op jit(solution)/shard_map/dot_general | solution.py:74
  253.1 0.0 reduce-scatter.5.cloned.1.call-update
  253.1 0.0 copy-start.1
  253.1 344.8 %reduce-scatter.5.cloned.1.call-done = f32[256,12288]{1,0:T(8,128)} async-done(((f32[1024,12288]{1,0:T(8,128)}), f32[256,12288]{1,0:T(8,128)}) %reduce-scatter.5.cloned.1.call-update) | async-done | bytes 12582928 | tf_op jit(solution)/shard_map/reduce_scatter | solution.py:73
  597.9 0.0 copy-done.1
  (4 shorter events, 0.0 us)
Async XLA Ops:
  6.5 127.3 %copy-start = (f32[1,768,768]{2,1,0:T(8,128)S(1)}, f32[1,768,768]{2,1,0:T(8,128)}, u32[]{:S(2)}) copy-start(f32[1,768,768]{2,1,0:T(8,128)} %param.8) | copy-start | bytes 7077892
  6.5 103.9 %reduce-scatter.3.cloned.1.call-start = ((), (), s32[]{:S(2)}) async-start(), calls=%async_computation.2 | async-start | bytes 3538944 | tf_op jit(solution)/shard_map/reduce_scatter | solution.py:26
  33.0 0.7 copy-start.3
  33.0 79.7 %copy-start.2 = (s32[24]{0:T(128)S(1)}, s32[24]{0:T(128)}, u32[]{:S(2)}) copy-start(s32[24]{0:T(128)} %param.9) | copy-start | bytes 292
  33.1 98.5 %all-gather.5.cloned.1.call-start = ((), (), s32[]{:S(2)}) async-start(), calls=%async_computation.3 | async-start | bytes 1966080 | tf_op jit(solution)/shard_map/all_gather | solution.py:37
  112.7 43.8 %all-gather.9.cloned.1.call-start = ((), (), s32[]{:S(2)}) async-start(), calls=%async_computation.6 | async-start | bytes 1966080 | tf_op jit(solution)/shard_map/all_gather | solution.py:53
  113.5 23.5 %copy-start.4 = (s32[1,2]{1,0:T(1,128)S(1)}, s32[1,2]{1,0:T(1,128)}, u32[]{:S(2)}) copy-start(s32[1,2]{1,0:T(1,128)} %param.10) | copy-start | bytes 28
  136.7 86.1 %all-gather.7.cloned.1.call-start = ((), (), s32[]{:S(2)}) async-start(), calls=%async_computation.4 | async-start | bytes 1769472 | tf_op jit(solution)/shard_map/all_gather | solution.py:71
  178.2 419.7 %reduce-scatter.5.cloned.1.call-start = ((), (), s32[]{:S(2)}) async-start(), calls=%async_computation.5 | async-start | bytes 62914560 | tf_op jit(solution)/shard_map/reduce_scatter | solution.py:73
  253.1 344.9 %copy-start.1 = (f32[1,768,768]{2,1,0:T(8,128)S(1)}, f32[1,768,768]{2,1,0:T(8,128)}, u32[]{:S(2)}) copy-start(f32[1,768,768]{2,1,0:T(8,128)} %param.8) | copy-start | bytes 7077892
Sparse Core Ops, SparseCore 0:
  33.2 77.1 reduce-scatter.2
  112.8 18.7 all-gather.4
  136.8 19.6 all-gather.8
  178.4 44.4 all-gather.6
  253.2 344.6 reduce-scatter.4
where the time goes:
time: 605 us; the launch traced here: 604 us
  waiting for transfers between devices  502 us (83%)
  matrix products  68.5 us (11%)
  between operations  13.3 us (2%)
  local copies, waits for them, and re-layouts  9.05 us (1%)
  blocking collectives  8.58 us (1%)
    reduce_scatter x1, waiting for transfers between devices, body(): lax.psum_scatter(gain_factor * jnp.dot(all_loads, panel, preferred_elemen...  345 us
    reduce_scatter x1, waiting for transfers between devices, body(): lax.psum_scatter(lax.dot_general(surface, panel, (((0,), (1,)), ((), ()))...  76.6 us
    all_gather x1, waiting for transfers between devices, body(): all_loads = lax.all_gather(updated, 'col', axis=0, tiled=True)  44.3 us
    dot_general x1, matrix products, body(): jnp.dot(all_loads, panel, preferred_element_type=jnp.float32)  30.3 us
    dot_general x1, matrix products, body(): lax.dot_general(surface, panel, (((0,), (1,)), ((), ())), preferred_eleme...  26.5 us
    all_gather x1, waiting for transfers between devices, body(): neighbours = lax.all_gather(traces[None], 'row', axis=0, tiled=True)  18.3 us
    all_gather x1, waiting for transfers between devices, body(): every_block = lax.all_gather(blocks, 'row', axis=1, tiled=True)  18 us
  transfers between devices with their start and end apart: 5, of which 5 were waited for; matrix products, arithmetic and copies ran while one was open for 0% of the time, Pallas kernels for 0%

commit v1 on v0

--- a/solution.py
+++ b/solution.py
@@ -68,7 +68,12 @@
     updated = (
         jnp.take(every_trace, own_slots, axis=1) * own_pattern[None].astype(jnp.bfloat16)
     ).reshape(load_share, order_rows)
-    all_loads = lax.all_gather(updated, "col", axis=0, tiled=True)
+    ring = [updated]
+    for hop in range(7):
+        ring.append(lax.ppermute(ring[-1], "col", [(dev, (dev + 1) % 8) for dev in range(8)]))
+    all_loads = jnp.roll(
+        jnp.concatenate(ring[::-1], axis=0), (lax.axis_index("col") + 1) * ring[0].shape[0], axis=0
+    )
     gain_factor = math.sqrt(column_count * col_total / (order_rows * row_total))
     return lax.psum_scatter(
         gain_factor * jnp.dot(all_loads, panel, preferred_element_type=jnp.float32),

time: 605 us -> 630 us (1.041)
  waiting for transfers between devices: 502 us -> 516 us
  local copies, waits for them, and re-layouts: 9.05 us -> 20.1 us
    ppermute x0 -> x7, waiting for transfers between devices: none -> 59.9 us  [body(): lax.ppermute(ring[-1], 'col', [(dev, (dev + 1) % 8) for dev in range(8)])]
    all_gather x1 -> x0, waiting for transfers between devices: 44.3 us -> none  [body(): all_loads = lax.all_gather(updated, 'col', axis=0, tiled=True)]
    unnamed x10 -> x25, local copies, waits for them, and re-layouts: 0.59 us -> 10.9 us
  transfers between devices with their start and end apart: 5 -> 11, of which waited for: 5 -> 11; matrix products, arithmetic and copies ran while one was open for 0% -> 0% of each run, Pallas kernels for 0% -> 0%
where the time goes in v1:
time: 630 us
  waiting for transfers between devices  516 us (82%)
  matrix products  68.6 us (11%)
  local copies, waits for them, and re-layouts  20.1 us (3%)
  between operations  13.3 us (2%)
  blocking collectives  8.58 us (1%)
    reduce_scatter x1, waiting for transfers between devices, body(): lax.psum_scatter(gain_factor * jnp.dot(all_loads, panel, preferred_elemen...  343 us
    reduce_scatter x1, waiting for transfers between devices, body(): lax.psum_scatter(lax.dot_general(surface, panel, (((0,), (1,)), ((), ()))...  76.6 us
    ppermute x7, waiting for transfers between devices, body(): lax.ppermute(ring[-1], 'col', [(dev, (dev + 1) % 8) for dev in range(8)])  59.9 us
    dot_general x1, matrix products, body(): jnp.dot(all_loads, panel, preferred_element_type=jnp.float32)  30.4 us
    dot_general x1, matrix products, body(): lax.dot_general(surface, panel, (((0,), (1,)), ((), ())), preferred_eleme...  26.5 us
    all_gather x1, waiting for transfers between devices, body(): neighbours = lax.all_gather(traces[None], 'row', axis=0, tiled=True)  18.3 us
    all_gather x1, waiting for transfers between devices, body(): every_block = lax.all_gather(blocks, 'row', axis=1, tiled=True)  18 us
  transfers between devices with their start and end apart: 11, of which 11 were waited for; matrix products, arithmetic and copies ran while one was open for 0% of the time, Pallas kernels for 0%

profile of v1, /device:TPU:0, one launch (start us, length us, event | category | flops | bytes accessed | tf_op | source)
XLA Modules:
  0.0 629.9 jit_solution(14632227334438595398)
XLA Ops:
  6.5 26.5 %fusion.27 = f32[1024,768]{1,0:T(8,128)} fusion(bf16[12288,1024]{1,0:T(8,128)(2,1)} %param.7, bf16[768,12288]{1,0:T(8,128)(2,1)} %param.6), kind=kOutput, calls=%fused_computation.58 | convolution fusion | flops 19327352832 | bytes 47185920 | tf_op jit(solution)/shard_map/dot_general | solution.py:27
  33.0 0.0 reduce-scatter.3.cloned.1.call-update
  33.1 0.0 all-gather.4.cloned.1.call-start
  33.1 0.6 copy-done.3
  33.7 0.1 dynamic-slice
  33.8 0.1 convert_bitcast_fusion
  33.8 76.6 %reduce-scatter.3.cloned.1.call-done = f32[128,768]{1,0:T(8,128)} async-done(((f32[1024,768]{1,0:T(8,128)}), f32[128,768]{1,0:T(8,128)}) %reduce-scatter.3.cloned.1.call-update) | async-done | bytes 393232 | tf_op jit(solution)/shard_map/reduce_scatter | solution.py:26
  110.4 1.1 copy.21
  111.6 0.2 broadcast_multiply_fusion.1
  111.7 0.9 copy.22
  112.7 0.0 all-gather.4.cloned.1.call-update
  112.7 0.0 all-gather.6.cloned.1.call-start
  112.8 0.6 scatter_custom_fusion
  113.4 0.1 compare_and_fusion
  113.5 18.0 %all-gather.4.cloned.1.call-done = f32[128,24,128]{2,0,1:T(8,128)} async-done(((f32[128,6,128]{2,0,1:T(8,128)}), f32[128,24,128]{2,0,1:T(8,128)}) %all-gather.4.cloned.1.call-update) | async-done | bytes 1572880 | tf_op jit(solution)/shard_map/all_gather | solution.py:37
  131.6 2.0 gather_fusion
  133.6 0.1 broadcast_select_fusion
  133.7 0.2 copy.23
  133.8 2.8 broadcast_multiply_fusion
  136.7 0.0 all-gather.6.cloned.1.call-update
  136.7 0.2 reduce-scatter.5.cloned.1.call-start
  136.9 0.1 compare_and_fusion.1
  137.0 0.7 fusion.21
  137.7 0.1 broadcast_bitcast_fusion
  137.8 0.1 broadcast_bitcast_fusion.1
  137.9 0.2 copy.24
  138.0 0.2 bitcast_select_fusion
  138.2 18.3 %all-gather.6.cloned.1.call-done = f32[512,768]{1,0:T(8,128)} async-done(((f32[128,768]{1,0:T(8,128)}), f32[512,768]{1,0:T(8,128)}) %all-gather.6.cloned.1.call-update) | async-done | bytes 1572880 | tf_op jit(solution)/shard_map/all_gather | solution.py:53
  156.5 5.7 fusion.4
  162.2 1.2 copy.29
  163.4 3.2 fusion.13
  166.6 1.1 copy.25
  167.7 0.2 copy.26
  167.9 8.6 %all_gather.11 = bf16[128,24,128]{2,0,1:T(8,128)(2,1)S(1)} all-gather(bf16[128,6,128]{2,0,1:T(8,128)(2,1)S(1)} %copy.26), channel_id=1, replica_groups=mesh['row'=4,'col'=8] {'row'}, dimensions={1}, use_global_device_ids=true | all-gather | bytes 983040 | tf_op jit(solution)/shard_map/all_gather | solution.py:66
  176.5 0.6 gather_fusion.1
  177.1 0.2 copy.27
  177.3 0.3 fusion.18
  177.5 1.5 collective-permute-start
  179.1 8.4 %collective-permute-done = bf16[128,768]{0,1:T(8,128)(2,1)S(1)} collective-permute-done((bf16[128,768]{0,1:T(8,128)(2,1)S(1)}, bf16[128,768]{0,1:T(8,128)(2,1)S(1)}, u32[]{:S(2)}, u32[]{:S(2)}) %collective-permute-start) | collective-permute-done | bytes 196640 | tf_op jit(solution)/shard_map/ppermute | solution.py:73
  187.4 9.0 %collective-permute-done.1 = bf16[128,768]{0,1:T(8,128)(2,1)S(1)} collective-permute-done((bf16[128,768]{0,1:T(8,128)(2,1)S(1)}, bf16[128,768]{0,1:T(8,128)(2,1)S(1)}, u32[]{:S(2)}, u32[]{:S(2)}) %collective-permute-start.1) | collective-permute-done | bytes 196640 | tf_op jit(solution)/shard_map/ppermute | solution.py:73
  196.4 8.4 %collective-permute-done.2 = bf16[128,768]{0,1:T(8,128)(2,1)S(1)} collective-permute-done((bf16[128,768]{0,1:T(8,128)(2,1)S(1)}, bf16[128,768]{0,1:T(8,128)(2,1)S(1)}, u32[]{:S(2)}, u32[]{:S(2)}) %collective-permute-start.2) | collective-permute-done | bytes 196640 | tf_op jit(solution)/shard_map/ppermute | solution.py:73
  204.8 8.4 %collective-permute-done.3 = bf16[128,768]{0,1:T(8,128)(2,1)S(1)} collective-permute-done((bf16[128,768]{0,1:T(8,128)(2,1)S(1)}, bf16[128,768]{0,1:T(8,128)(2,1)S(1)}, u32[]{:S(2)}, u32[]{:S(2)}) %collective-permute-start.3) | collective-permute-done | bytes 196640 | tf_op jit(solution)/shard_map/ppermute | solution.py:73
  213.2 8.4 %collective-permute-done.4 = bf16[128,768]{0,1:T(8,128)(2,1)S(1)} collective-permute-done((bf16[128,768]{0,1:T(8,128)(2,1)S(1)}, bf16[128,768]{0,1:T(8,128)(2,1)S(1)}, u32[]{:S(2)}, u32[]{:S(2)}) %collective-permute-start.4) | collective-permute-done | bytes 196640 | tf_op jit(solution)/shard_map/ppermute | solution.py:73
  221.5 9.0 %collective-permute-done.5 = bf16[128,768]{0,1:T(8,128)(2,1)S(1)} collective-permute-done((bf16[128,768]{0,1:T(8,128)(2,1)S(1)}, bf16[128,768]{0,1:T(8,128)(2,1)S(1)}, u32[]{:S(2)}, u32[]{:S(2)}) %collective-permute-start.5) | collective-permute-done | bytes 196640 | tf_op jit(solution)/shard_map/ppermute | solution.py:73
  230.6 8.4 %collective-permute-done.6 = bf16[128,768]{0,1:T(8,128)(2,1)S(1)} collective-permute-done((bf16[128,768]{0,1:T(8,128)(2,1)S(1)}, bf16[128,768]{0,1:T(8,128)(2,1)S(1)}, u32[]{:S(2)}, u32[]{:S(2)}) %collective-permute-start.6) | collective-permute-done | bytes 196640 | tf_op jit(solution)/shard_map/ppermute | solution.py:73
  238.9 0.7 constant_dynamic-update-slice_fusion.15
  239.6 0.7 constant_dynamic-update-slice_fusion.14
  240.3 0.7 constant_dynamic-update-slice_fusion.13
  241.0 0.7 constant_dynamic-update-slice_fusion.12
  241.7 0.7 constant_dynamic-update-slice_fusion.11
  242.4 0.7 constant_dynamic-update-slice_fusion.10
  243.1 0.7 constant_dynamic-update-slice_fusion.9
  243.8 0.7 constant_dynamic-update-slice_fusion.8
  244.5 0.7 constant_dynamic-update-slice_fusion.7
  245.2 0.7 constant_dynamic-update-slice_fusion.6
  245.8 0.7 constant_dynamic-update-slice_fusion.5
  246.5 0.7 constant_dynamic-update-slice_fusion.4
  247.2 0.7 constant_dynamic-update-slice_fusion.3
  247.9 0.7 constant_dynamic-update-slice_fusion.2
  248.6 0.7 constant_dynamic-update-slice_fusion.1
  249.3 0.7 constant_dynamic-update-slice_fusion
  250.0 30.4 %convolution_multiply_fusion = f32[1024,12288]{1,0:T(8,128)} fusion(bf16[768,12288]{1,0:T(8,128)(2,1)} %param.6, bf16[2048,768]{0,1:T(8,128)(2,1)} %constant_dynamic-update-slice_fusion, s32[]{:T(128)S(6)} %select_n.60), kind=kOutput, calls=%fused_computation.3 | convolution fusion | flops 19339935744 | bytes 70778880 | tf_op jit(solution)/shard_map/dot_general | solution.py:79
  280.3 0.0 reduce-scatter.5.cloned.1.call-update
  280.4 343.0 %reduce-scatter.5.cloned.1.call-done = f32[256,12288]{1,0:T(8,128)} async-done(((f32[1024,12288]{1,0:T(8,128)}), f32[256,12288]{1,0:T(8,128)}) %reduce-scatter.5.cloned.1.call-update) | async-done | bytes 12582928 | tf_op jit(solution)/shard_map/reduce_scatter | solution.py:78
  (20 shorter events, 0.1 us)
Async XLA Ops:
  6.5 127.3 %copy-start = (f32[1,768,768]{2,1,0:T(8,128)S(1)}, f32[1,768,768]{2,1,0:T(8,128)}, u32[]{:S(2)}) copy-start(f32[1,768,768]{2,1,0:T(8,128)} %param.8) | copy-start | bytes 7077892
  6.5 103.9 %reduce-scatter.3.cloned.1.call-start = ((), (), s32[]{:S(2)}) async-start(), calls=%async_computation.2 | async-start | bytes 3538944 | tf_op jit(solution)/shard_map/reduce_scatter | solution.py:26
  33.0 0.7 copy-start.3
  33.0 79.7 %copy-start.2 = (s32[24]{0:T(128)S(1)}, s32[24]{0:T(128)}, u32[]{:S(2)}) copy-start(s32[24]{0:T(128)} %param.9) | copy-start | bytes 292
  33.1 98.5 %all-gather.4.cloned.1.call-start = ((), (), s32[]{:S(2)}) async-start(), calls=%async_computation.3 | async-start | bytes 1966080 | tf_op jit(solution)/shard_map/all_gather | solution.py:37
  112.7 43.8 %all-gather.6.cloned.1.call-start = ((), (), s32[]{:S(2)}) async-start(), calls=%async_computation.5 | async-start | bytes 1966080 | tf_op jit(solution)/shard_map/all_gather | solution.py:53
  113.5 23.5 %copy-start.4 = (s32[1,2]{1,0:T(1,128)S(1)}, s32[1,2]{1,0:T(1,128)}, u32[]{:S(2)}) copy-start(s32[1,2]{1,0:T(1,128)} %param.10) | copy-start | bytes 28
  136.7 486.6 %reduce-scatter.5.cloned.1.call-start = ((), (), s32[]{:S(2)}) async-start(), calls=%async_computation.4 | async-start | bytes 62914560 | tf_op jit(solution)/shard_map/reduce_scatter | solution.py:78
  177.5 9.9 %collective-permute-start = (bf16[128,768]{0,1:T(8,128)(2,1)S(1)}, bf16[128,768]{0,1:T(8,128)(2,1)S(1)}, u32[]{:S(2)}, u32[]{:S(2)}) collective-permute-start(bf16[128,768]{0,1:T(8,128)(2,1)S(1)} %fusion.18), channel_id=1, source_target_pairs={{0,1},{1,2},{2,3},{3,4},{4,5},{5,6},{6,7},{7,0},{8,9},{9,10},{10,1... | collective-permute-start | bytes 589832 | tf_op jit(solution)/shard_map/ppermute | solution.py:73
  187.4 9.0 %collective-permute-start.1 = (bf16[128,768]{0,1:T(8,128)(2,1)S(1)}, bf16[128,768]{0,1:T(8,128)(2,1)S(1)}, u32[]{:S(2)}, u32[]{:S(2)}) collective-permute-start(bf16[128,768]{0,1:T(8,128)(2,1)S(1)} %collective-permute-done), channel_id=1, source_target_pairs={{0,1},{1,2},{2,3},{3,4},{4,5},{5,6},{6,7},{7,0},{8,9},{9,10},{10,1... | collective-permute-start | bytes 589832 | tf_op jit(solution)/shard_map/ppermute | solution.py:73
  196.4 8.4 %collective-permute-start.2 = (bf16[128,768]{0,1:T(8,128)(2,1)S(1)}, bf16[128,768]{0,1:T(8,128)(2,1)S(1)}, u32[]{:S(2)}, u32[]{:S(2)}) collective-permute-start(bf16[128,768]{0,1:T(8,128)(2,1)S(1)} %collective-permute-done.1), channel_id=1, source_target_pairs={{0,1},{1,2},{2,3},{3,4},{4,5},{5,6},{6,7},{7,0},{8,9},{9,10},{10,1... | collective-permute-start | bytes 589832 | tf_op jit(solution)/shard_map/ppermute | solution.py:73
  204.8 8.4 %collective-permute-start.3 = (bf16[128,768]{0,1:T(8,128)(2,1)S(1)}, bf16[128,768]{0,1:T(8,128)(2,1)S(1)}, u32[]{:S(2)}, u32[]{:S(2)}) collective-permute-start(bf16[128,768]{0,1:T(8,128)(2,1)S(1)} %collective-permute-done.2), channel_id=1, source_target_pairs={{0,1},{1,2},{2,3},{3,4},{4,5},{5,6},{6,7},{7,0},{8,9},{9,10},{10,1... | collective-permute-start | bytes 589832 | tf_op jit(solution)/shard_map/ppermute | solution.py:73
  213.2 8.4 %collective-permute-start.4 = (bf16[128,768]{0,1:T(8,128)(2,1)S(1)}, bf16[128,768]{0,1:T(8,128)(2,1)S(1)}, u32[]{:S(2)}, u32[]{:S(2)}) collective-permute-start(bf16[128,768]{0,1:T(8,128)(2,1)S(1)} %collective-permute-done.3), channel_id=1, source_target_pairs={{0,1},{1,2},{2,3},{3,4},{4,5},{5,6},{6,7},{7,0},{8,9},{9,10},{10,1... | collective-permute-start | bytes 589832 | tf_op jit(solution)/shard_map/ppermute | solution.py:73
  221.5 9.0 %collective-permute-start.5 = (bf16[128,768]{0,1:T(8,128)(2,1)S(1)}, bf16[128,768]{0,1:T(8,128)(2,1)S(1)}, u32[]{:S(2)}, u32[]{:S(2)}) collective-permute-start(bf16[128,768]{0,1:T(8,128)(2,1)S(1)} %collective-permute-done.4), channel_id=1, source_target_pairs={{0,1},{1,2},{2,3},{3,4},{4,5},{5,6},{6,7},{7,0},{8,9},{9,10},{10,1... | collective-permute-start | bytes 589832 | tf_op jit(solution)/shard_map/ppermute | solution.py:73
  230.6 8.4 %collective-permute-start.6 = (bf16[128,768]{0,1:T(8,128)(2,1)S(1)}, bf16[128,768]{0,1:T(8,128)(2,1)S(1)}, u32[]{:S(2)}, u32[]{:S(2)}) collective-permute-start(bf16[128,768]{0,1:T(8,128)(2,1)S(1)} %collective-permute-done.5), channel_id=1, source_target_pairs={{0,1},{1,2},{2,3},{3,4},{4,5},{5,6},{6,7},{7,0},{8,9},{9,10},{10,1... | collective-permute-start | bytes 589832 | tf_op jit(solution)/shard_map/ppermute | solution.py:73
  280.4 343.0 %copy-start.1 = (f32[1,768,768]{2,1,0:T(8,128)S(1)}, f32[1,768,768]{2,1,0:T(8,128)}, u32[]{:S(2)}) copy-start(f32[1,768,768]{2,1,0:T(8,128)} %param.8) | copy-start | bytes 7077892
Sparse Core Ops, SparseCore 0:
  33.2 77.1 reduce-scatter.2
  112.8 18.7 all-gather.3
  136.8 19.6 all-gather.5
  280.5 342.8 reduce-scatter.4
